TPU v7x, 32 devices: a whole 2x2x4 slice. The times are simulated.
32 devices in a mesh: rows: 8 (over y, x, core), probe: 4 (over z).
Axes of the slice: x: 2, y: 2, z: 4, core: 2. Of those that a mesh axis runs over, the one named last changes fastest.
Arguments:
- points: float32 [64, 3, 128], P('rows'), may hold values from 0 to 1
- observations: float32 [64, 128], P('rows'), may hold values from -6 to 6
- probes: float32 [64, 64, 128], P('rows', 'probe'), may hold values from -150 to 150
- neighbours: int32 [64, 3], P('rows'), may hold values from 0 to 63, as said below
- block_position: int32 [64], P('rows'), may hold values from 0 to 63, as said below
Outputs:
- whitened: float32 [64, 128], P('rows')
- block_terms: float32 [64], P('rows')
- tridiagonal: float32 [64, 3], P('probe')
- remainder: float32 [64, 64, 128], P('rows', 'probe')
Inputs may be any that keep to these rules, and one draw needn't show every extreme that they name: block_position is a permutation of the block ids; the block with id i sits at position block_position[i], on index block_position[i] // 8 of rows. neighbours[b] lists three block ids, which may repeat and may name the block at b itself. Over the 24 references of the blocks of one index of rows, the positions of the named blocks fall at most 6 times on the blocks of any one index of rows, and exactly 6 times on those of some index, for every index.
All inputs are finite; a program needn't handle non-finite values.
Results may differ from a plain program's by a relative error of at most 0.0003.
Values sent between devices are 32-bit elements; how exact they have to be, the bound alone decides.
A program may use at most 64 MiB of HBM per device.

v0:
```python
import math

import jax
import jax.numpy as jnp
from jax import lax
from jax.experimental import pallas as pl
from jax.experimental.pallas import tpu as pltpu
from jax.sharding import PartitionSpec as P

length_scale = 0.3
nugget = 0.25
epsilon = 1e-06
highest = lax.Precision.HIGHEST
chunk = 8
width = 4


def dot(left, right):
    return jnp.dot(left, right, precision=highest, preferred_element_type=jnp.float32)


def dot_nt(left, right):
    return lax.dot_general(
        left, right, (((1,), (1,)), ((), ())), precision=highest,
        preferred_element_type=jnp.float32,
    )


def pivot_inverse(rows, e):
    rows = list(rows)
    e = [list(r) for r in e]
    for k in range(width):
        inv = 1.0 / e[k][k]
        rows[k] = rows[k] * inv
        for n in range(k + 1, width):
            e[k][n] = e[k][n] * inv
        for m in range(width):
            if m != k:
                f = e[m][k]
                rows[m] = rows[m] - f * rows[k]
                for n in range(k + 1, width):
                    e[m][n] = e[m][n] - f * e[k][n]
    return rows


def pivot_factor(rows, e):
    e = [list(r) for r in e]
    y = list(rows)
    inv = []
    product = None
    for k in range(width):
        d = e[k][k]
        s = lax.rsqrt(d)
        s = s * (1.5 - 0.5 * d * s * s)
        inv.append(s)
        product = s if product is None else product * s
        y[k] = y[k] * s
        for m in range(k + 1, width):
            e[m][k] = e[m][k] * s
        for m in range(k + 1, width):
            y[m] = y[m] - e[m][k] * y[k]
            for n in range(k + 1, m + 1):
                e[m][n] = e[m][n] - e[m][k] * e[n][k]
    r = list(y)
    for k in reversed(range(width)):
        for m in range(k + 1, width):
            r[k] = r[k] - e[m][k] * r[m]
        r[k] = r[k] * inv[k]
    return y, r, jnp.log(product)


def sweep(mats, factor):
    count = len(mats[0])
    shape = mats[0][0].shape
    lane = lax.broadcasted_iota(jnp.int32, shape, 1)
    sub = lax.broadcasted_iota(jnp.int32, shape, 0)

    def full(x):
        return jnp.broadcast_to(x, shape)

    def step(t, carry):
        mats, logs = carry
        mats = [list(m) for m in mats]
        logs = list(logs)
        for o in range(0, chunk, width):
            picked = (lane >= o) & (lane < o + width)
            for b in range(len(mats)):
                chunks = mats[b]
                top = chunks[0]
                cols = [full(top[:, o + k : o + k + 1]) for k in range(width)]
                rows = [full(top[o + k : o + k + 1, :]) for k in range(width)]
                e = [[full(cols[k][o + m : o + m + 1, :]) for k in range(width)] for m in range(width)]
                rows = [
                    jnp.where(lane == o + k, 1.0, jnp.where(picked, 0.0, rows[k]))
                    for k in range(width)
                ]
                if factor:
                    kept, r, term = pivot_factor(rows, e)
                    logs[b] = logs[b] + term
                else:
                    r = pivot_inverse(rows, e)
                    kept = r
                for p in range(count):
                    old = chunks[p]
                    if p:
                        cols = [full(old[:, o + k : o + k + 1]) for k in range(width)]
                    new = jnp.where(picked, 0.0, old)
                    for k in range(width):
                        new = new - cols[k] * r[k]
                    if p == 0:
                        if factor:
                            new = jnp.where(sub >= o + width, new, old)
                        for k in range(width):
                            new = jnp.where(sub == o + k, kept[k], new)
                    elif factor:
                        new = jnp.where(t + p < count, new, old)
                    chunks[p] = new
        turned = []
        for chunks in mats:
            chunks = [pltpu.roll(c, shape[1] - chunk, 1) for c in chunks]
            turned.append(tuple(chunks[1:] + chunks[:1]))
        return tuple(turned), tuple(logs)

    zero = jnp.zeros(shape, jnp.float32)
    return lax.fori_loop(0, count, step, (mats, tuple(zero for _ in mats)))


def factor_kernel(rows_ref, cols_ref, vals_ref, g_ref, w_ref, t_ref, a_ref):
    nb = rows_ref.shape[0]
    bs = g_ref.shape[1]

    def part(i):
        return slice(i * bs, (i + 1) * bs)

    def load(j):
        return tuple(
            tuple(
                a_ref[b, j * bs + i * chunk : j * bs + (i + 1) * chunk, part(j)]
                for i in range(bs // chunk)
            )
            for b in range(nb)
        )

    same = lax.broadcasted_iota(jnp.int32, (bs, bs), 0) == lax.broadcasted_iota(
        jnp.int32, (bs, bs), 1
    )
    below = lax.broadcasted_iota(jnp.int32, (bs, bs), 0) >= lax.broadcasted_iota(
        jnp.int32, (bs, bs), 1
    )
    for b in range(nb):
        for i in range(4):
            for k in range(i + 1):
                dist_sq = None
                for c in range(3):
                    off = cols_ref[b, part(i), c : c + 1] - rows_ref[b, c : c + 1, part(k)]
                    dist_sq = off * off if dist_sq is None else dist_sq + off * off
                value = 1.0 / (1.0 + dist_sq * (1.0 / (length_scale * length_scale)))
                if i == k:
                    value = value + jnp.where(same, nugget, 0.0)
                a_ref[b, part(i), part(k)] = value
    for j in range(3):
        inverse, _ = sweep(load(j), False)
        for b in range(nb):
            p = jnp.concatenate(inverse[b], axis=0)
            rest = a_ref[b, (j + 1) * bs :, part(j)]
            scaled = dot(rest, p)
            for i in range(j + 1, 4):
                row = scaled[(i - j - 1) * bs : (i - j) * bs]
                a_ref[b, part(i), (j + 1) * bs : (i + 1) * bs] -= dot_nt(
                    row, rest[: (i - j) * bs]
                )
            a_ref[b, (j + 1) * bs :, part(j)] = scaled
    low, logs = sweep(load(3), True)
    for b in range(nb):
        low_inv = jnp.where(below, jnp.concatenate(low[b], axis=0), 0.0)
        x2 = a_ref[b, part(3), part(2)]
        x1 = a_ref[b, part(3), part(1)] - dot(x2, a_ref[b, part(2), part(1)])
        x0 = (
            a_ref[b, part(3), part(0)]
            - dot(x1, a_ref[b, part(1), part(0)])
            - dot(x2, a_ref[b, part(2), part(0)])
        )
        g_ref[b, :, part(3)] = low_inv
        for i, x in enumerate((x0, x1, x2)):
            g_ref[b, :, part(i)] = -dot(low_inv, x)
        w = dot_nt(vals_ref[b], g_ref[b])
        w_ref[b] = w
        square = jnp.sum(w[:1] * w[:1], axis=1, keepdims=True)
        t_ref[b] = (logs[b] - 0.5 * square) * (1.0 / bs) - 0.5 * math.log(2.0 * math.pi)


def factor_blocks(points, values):
    nb, dims, order = points.shape
    bs = order // 4
    rows = jnp.pad(points, ((0, 0), (0, chunk - dims), (0, 0)))
    cols = jnp.swapaxes(points, 1, 2)
    vals = jnp.broadcast_to(values[:, None], (nb, chunk, order))
    g, w, t = pl.pallas_call(
        factor_kernel,
        out_shape=(
            jax.ShapeDtypeStruct((nb, bs, order), jnp.float32),
            jax.ShapeDtypeStruct((nb, chunk, bs), jnp.float32),
            jax.ShapeDtypeStruct((nb, chunk, bs), jnp.float32),
        ),
        scratch_shapes=[pltpu.VMEM((nb, order, order), jnp.float32)],
    )(rows, cols, vals)
    return g, w[:, 0], t[:, 0, 0]


def local_inner(left, right):
    return jnp.sum(left * right, axis=(0, 2))


def body(points, observations, probes, neighbours, block_position):
    row_count = lax.axis_size("rows")
    blocks = points.shape[0]
    block_size = points.shape[2]
    probe_cols = probes.shape[1]
    cells = blocks * row_count * block_size
    references = 3 * blocks
    capacity = max(2, 6 * blocks // row_count)
    slot_count = row_count * capacity
    whole_position = lax.all_gather(block_position, "rows", axis=0, tiled=True)
    all_blocks = whole_position.shape[0]
    block_ids = jnp.arange(all_blocks, dtype=jnp.int32)
    near_ids = neighbours.reshape(references)
    near_rows = jnp.sum(
        jnp.where(near_ids[:, None] == block_ids[None, :], whole_position[None, :], 0), axis=1
    )
    coord_rows = points.reshape(blocks, 3 * block_size)
    owners = near_rows // blocks
    local_rows = near_rows % blocks
    ref_index = jnp.arange(references, dtype=jnp.int32)
    earlier = (owners[:, None] == owners[None, :]) & (ref_index[:, None] > ref_index[None, :])
    slot_index = owners * capacity + jnp.sum(earlier.astype(jnp.int32), axis=1)
    slot_hits = slot_index[:, None] == jnp.arange(slot_count, dtype=jnp.int32)[None, :]
    to_slot = slot_hits.astype(jnp.float32)
    wanted = jnp.sum(jnp.where(slot_hits, local_rows[:, None] + 1, 0), axis=0) - 1
    requested = lax.all_to_all(
        wanted.reshape(row_count, capacity), "rows", split_axis=0, concat_axis=0, tiled=True
    ).reshape(slot_count)
    picked = (requested[:, None] == jnp.arange(blocks, dtype=jnp.int32)[None, :]).astype(
        jnp.float32
    )

    def select_rows(source):
        return jnp.dot(picked, source, precision=highest).reshape(
            row_count, capacity, source.shape[1]
        )

    def to_refs(incoming):
        return jnp.dot(to_slot, incoming.reshape(slot_count, incoming.shape[2]), precision=highest)

    def fetch_rows(source):
        return to_refs(
            lax.all_to_all(select_rows(source), "rows", split_axis=0, concat_axis=0, tiled=True)
        )

    def return_terms(term_rows):
        outgoing = jnp.einsum("rs,rf->sf", to_slot, term_rows, precision=highest).reshape(
            row_count, capacity, term_rows.shape[1]
        )
        incoming = lax.all_to_all(outgoing, "rows", split_axis=0, concat_axis=0, tiled=True)
        return jnp.einsum(
            "sb,sf->bf", picked, incoming.reshape(slot_count, term_rows.shape[1]), precision=highest
        )

    incoming = (
        lax.all_to_all(select_rows(coord_rows), "rows", split_axis=0, concat_axis=0, tiled=True),
        lax.all_to_all(select_rows(observations), "rows", split_axis=0, concat_axis=0, tiled=True),
    )
    near_coords = to_refs(incoming[0])
    near_values = to_refs(incoming[1])
    near_points = near_coords.reshape(blocks, 3, 3, block_size)
    near_obs = near_values.reshape(blocks, 3, block_size)
    point_sets = jnp.concatenate([jnp.swapaxes(near_points, 1, 2), points[:, :, None]], axis=2)
    value_sets = jnp.concatenate([near_obs, observations[:, None]], axis=1)
    per_device = blocks // lax.axis_size("probe")
    first_block = lax.axis_index("probe") * per_device
    conditioner, whitened, block_terms = factor_blocks(
        lax.dynamic_slice_in_dim(
            point_sets.reshape(blocks, 3, 4 * block_size), first_block, per_device, 0
        ),
        lax.dynamic_slice_in_dim(
            value_sets.reshape(blocks, 4 * block_size), first_block, per_device, 0
        ),
    )
    conditioner, whitened, block_terms = (
        lax.all_gather(conditioner, "probe", axis=0, tiled=True),
        lax.all_gather(whitened, "probe", axis=0, tiled=True),
        lax.all_gather(block_terms, "probe", axis=0, tiled=True),
    )
    cond_four = conditioner.reshape(blocks, block_size, 4, block_size)

    def apply_operator(vector):
        near_vec = fetch_rows(vector.reshape(blocks, probe_cols * block_size)).reshape(
            blocks, 3, probe_cols, block_size
        )
        stacked = jnp.concatenate([near_vec, vector[:, None]], axis=1)
        projected = jnp.einsum("bjpm,bkjm->bpk", stacked, cond_four, precision=highest)
        spread = jnp.einsum("bpk,bkjm->bjpm", projected, cond_four, precision=highest)
        returned = return_terms(spread[:, :3].reshape(references, probe_cols * block_size))
        return spread[:, 3] + returned.reshape(blocks, probe_cols, block_size)

    square_sum = lax.psum(local_inner(probes, probes), "rows")
    probe_scale = jnp.sqrt(square_sum / cells + epsilon)
    basis_one = probes / probe_scale[None, :, None]
    image_one = apply_operator(basis_one)
    alpha_one = lax.psum(local_inner(basis_one, image_one), "rows") / cells
    residue = image_one - alpha_one[None, :, None] * basis_one
    beta_one = jnp.sqrt(lax.psum(local_inner(residue, residue), "rows") / cells + epsilon)
    basis_two = residue / beta_one[None, :, None]
    image_two = apply_operator(basis_two)
    alpha_two = lax.psum(local_inner(basis_two, image_two), "rows") / cells
    remainder = (
        image_two - alpha_two[None, :, None] * basis_two - beta_one[None, :, None] * basis_one
    )
    tridiagonal = jnp.stack([alpha_one, beta_one, alpha_two], axis=1)
    return (whitened, block_terms, tridiagonal, remainder)


def solution(mesh):
    placed = (
        P("rows", None, None),
        P("rows", None),
        P("rows", "probe", None),
        P("rows", None),
        P("rows"),
    )
    return jax.shard_map(
        body,
        mesh=mesh,
        in_specs=placed,
        out_specs=(P("rows", None), P("rows"), P("probe", None), P("rows", "probe", None)),
        check_vma=False,
    )
```

profile of v0, /device:TPU:9, one launch (start us, length us, event | category | flops | bytes accessed | tf_op | source)
XLA Modules:
  0.0 254.0 jit_solution(6971756980231862547)
XLA Ops:
  7.2 1.2 dynamic-slice
  9.1 0.9 dynamic-update-slice
  9.9 6.5 %all-reduce.1 = s32[64]{0:T(128)S(1)} all-reduce(s32[64]{0:T(128)S(1)} %dynamic-update-slice), channel_id=1, replica_groups=mesh['rows'=8,'probe'=4] {'rows'}, use_global_device_ids=true, to_apply=%add.1 | all-reduce | flops 64 | bytes 512
  18.4 5.4 %all-to-all-start = ((s32[8,1,6]{2,1,0:T(1,128)}), s32[8,1,6]{2,1,0:T(1,128)S(1)}, u32[]{:S(2)}, u32[]{:S(2)}) async-start(s32[8,1,6]{2,1,0:T(1,128)} %bitcast.4), calls=%async_computation | async-start | bytes 8192 | tf_op jit(solution)/shard_map/all_to_all | solution.py:239
  24.1 3.7 %all-to-all-done = s32[8,1,6]{2,1,0:T(1,128)S(1)} async-done(((s32[8,1,6]{2,1,0:T(1,128)}), s32[8,1,6]{2,1,0:T(1,128)S(1)}, u32[]{:S(2)}, u32[]{:S(2)}) %all-to-all-start) | async-done | bytes 224 | tf_op jit(solution)/shard_map/all_to_all | solution.py:239
  29.2 0.9 fusion.43
  30.7 3.9 %all-to-all-start.2 = ((f32[8,6,128]{2,1,0:T(8,128)}), f32[8,6,128]{2,1,0:T(8,128)S(1)}, u32[]{:S(2)}, u32[]{:S(2)}) async-start(f32[8,6,128]{2,1,0:T(8,128)} %reshape.289), calls=%async_computation.2 | async-start | bytes 65536 | tf_op jit(solution)/shard_map/all_to_all | solution.py:270
  34.7 1.5 fusion.23
  36.2 2.6 %all-to-all-done.2 = f32[8,6,128]{2,1,0:T(8,128)S(1)} async-done(((f32[8,6,128]{2,1,0:T(8,128)}), f32[8,6,128]{2,1,0:T(8,128)S(1)}, u32[]{:S(2)}, u32[]{:S(2)}) %all-to-all-start.2) | async-done | bytes 24608 | tf_op jit(solution)/shard_map/all_to_all | solution.py:270
  38.8 4.0 %all-to-all-start.1 = ((f32[8,6,384]{2,1,0:T(8,128)}), f32[8,6,384]{2,1,0:T(8,128)S(1)}, u32[]{:S(2)}, u32[]{:S(2)}) async-start(f32[8,6,384]{2,1,0:T(8,128)} %fusion.23), calls=%async_computation.1 | async-start | bytes 196608 | tf_op jit(solution)/shard_map/all_to_all | solution.py:269
  43.7 3.4 %all-to-all-done.1 = f32[8,6,384]{2,1,0:T(8,128)S(1)} async-done(((f32[8,6,384]{2,1,0:T(8,128)}), f32[8,6,384]{2,1,0:T(8,128)S(1)}, u32[]{:S(2)}, u32[]{:S(2)}) %all-to-all-start.1) | async-done | bytes 73760 | tf_op jit(solution)/shard_map/all_to_all | solution.py:269
  48.8 0.8 fusion.67.cols_ref
  51.0 50.9 %shard_map.84 = (f32[2,128,512]{2,1,0:T(8,128)}, f32[2,8,128]{2,1,0:T(8,128)}, f32[2,8,128]{2,1,0:T(8,128)}) custom-call(f32[2,8,512]{2,1,0:T(8,128)} %pad.4.clone.rows_ref, f32[2,512,3]{2,1,0:T(8,128)} %fusion.67.cols_ref, f32[2,8,512]{2,1,0:T(8,128)} %broadcast_in_dim.63.vals_ref), custom_call_target="tpu_custom_call" | custom-call | tf_op jit(solution)/shard_map/pallas_call | solution.py:198
  102.1 12.1 %psum.28 = f32[16]{0:T(128)S(1)} all-reduce(f32[16]{0:T(128)S(1)} %multiply_reduce_fusion.3), channel_id=1, replica_groups=mesh['rows'=8,'probe'=4] {'rows'}, use_global_device_ids=true, to_apply=%region_4.5 | all-reduce | flops 16 | bytes 128 | tf_op jit(solution)/shard_map/psum | solution.py:305
  114.2 1.2 fusion.15
  115.4 4.1 %all-to-all-start.3 = ((f32[8,6,2048]{2,1,0:T(8,128)}), f32[8,6,2048]{2,1,0:T(8,128)S(1)}, u32[]{:S(2)}, u32[]{:S(2)}) async-start(f32[8,6,2048]{2,1,0:T(8,128)} %fusion.15), calls=%async_computation.3 | async-start | bytes 1048576 | tf_op jit(solution)/shard_map/all_to_all | solution.py:256
  119.6 6.8 %all-to-all-done.3 = f32[8,6,2048]{2,1,0:T(8,128)S(1)} async-done(((f32[8,6,2048]{2,1,0:T(8,128)}), f32[8,6,2048]{2,1,0:T(8,128)S(1)}, u32[]{:S(2)}, u32[]{:S(2)}) %all-to-all-start.3) | async-done | bytes 393248 | tf_op jit(solution)/shard_map/all_to_all | solution.py:256
  126.8 18.7 %all-gather.4.cloned.1.call-done = f32[8,128,512]{2,1,0:T(8,128)} async-done(((f32[2,128,512]{2,1,0:T(8,128)}), f32[8,128,512]{2,1,0:T(8,128)}) %all-gather.4.cloned.1.call-update) | async-done | bytes 2097168 | tf_op jit(solution)/shard_map/all_gather | solution.py:289
  145.5 1.9 copy.101
  147.4 1.2 fusion.10
  148.5 1.9 fusion.55
  151.1 13.1 %all_to_all.36 = f32[8,6,2048]{2,1,0:T(8,128)S(1)} all-to-all(f32[8,6,2048]{2,1,0:T(8,128)S(1)} %fusion.19), channel_id=1, replica_groups=mesh['rows'=8,'probe'=4] {'rows'}, dimensions={0} | all-to-all | bytes 786432 | tf_op jit(solution)/shard_map/all_to_all | solution.py:263
  164.7 12.4 %psum.29 = f32[16]{0:T(128)S(1)} all-reduce(f32[16]{0:T(128)S(1)} %get-tuple-element.30), channel_id=1, replica_groups=mesh['rows'=8,'probe'=4] {'rows'}, use_global_device_ids=true, to_apply=%region_6.7 | all-reduce | flops 16 | bytes 128 | tf_op jit(solution)/shard_map/psum | solution.py:309
  177.4 11.8 %psum.30 = f32[16]{0:T(128)S(1)} all-reduce(f32[16]{0:T(128)S(1)} %multiply_reduce_fusion.1), channel_id=1, replica_groups=mesh['rows'=8,'probe'=4] {'rows'}, use_global_device_ids=true, to_apply=%region_8.9 | all-reduce | flops 16 | bytes 128 | tf_op jit(solution)/shard_map/psum | solution.py:311
  189.7 11.7 %all_to_all.37 = f32[8,6,2048]{2,1,0:T(8,128)S(1)} all-to-all(f32[8,6,2048]{2,1,0:T(8,128)S(1)} %fusion.13), channel_id=1, replica_groups=mesh['rows'=8,'probe'=4] {'rows'}, dimensions={0} | all-to-all | bytes 786432 | tf_op jit(solution)/shard_map/all_to_all | solution.py:256
  201.8 1.2 fusion.8
  202.9 1.9 fusion.56
  205.1 1.1 fusion.17
  206.2 4.6 %all-to-all-start.6 = ((f32[8,6,2048]{2,1,0:T(8,128)}), f32[8,6,2048]{2,1,0:T(8,128)S(1)}, u32[]{:S(2)}, u32[]{:S(2)}) async-start(f32[8,6,2048]{2,1,0:T(8,128)} %fusion.17), calls=%async_computation.6 | async-start | bytes 1048576 | tf_op jit(solution)/shard_map/all_to_all | solution.py:263
  213.1 8.6 %all-reduce.2 = f32[8]{0:T(128)} all-reduce(f32[8]{0:T(128)S(1)} %dynamic-update-slice.1), channel_id=3, replica_groups=mesh['rows'=8,'probe'=4] {'probe'}, use_global_device_ids=true, to_apply=%add.2 | all-reduce | flops 8 | bytes 64 | tf_op jit(solution)/shard_map/all_gather | solution.py:291
  222.4 6.7 %all-gather = f32[8,1,128]{2,1,0:T(1,128)S(1)} all-gather(f32[2,1,128]{2,1,0:T(1,128)S(1)} %slice.18), channel_id=2, replica_groups=mesh['rows'=8,'probe'=4] {'probe'}, dimensions={0}, use_global_device_ids=true | all-gather | bytes 5120 | tf_op jit(solution)/shard_map/all_gather | solution.py:290
  229.6 15.6 %psum.31 = f32[16]{0:T(128)S(1)} all-reduce(f32[16]{0:T(128)S(1)} %get-tuple-element.32), channel_id=1, replica_groups=mesh['rows'=8,'probe'=4] {'rows'}, use_global_device_ids=true, to_apply=%region_10.11 | all-reduce | flops 16 | bytes 128 | tf_op jit(solution)/shard_map/psum | solution.py:314
  (78 shorter events, 16.1 us)
Async XLA Ops:
  18.4 9.4 %all-to-all-start = ((s32[8,1,6]{2,1,0:T(1,128)}), s32[8,1,6]{2,1,0:T(1,128)S(1)}, u32[]{:S(2)}, u32[]{:S(2)}) async-start(s32[8,1,6]{2,1,0:T(1,128)} %bitcast.4), calls=%async_computation | async-start | bytes 8192 | tf_op jit(solution)/shard_map/all_to_all | solution.py:239
  30.7 8.0 %all-to-all-start.2 = ((f32[8,6,128]{2,1,0:T(8,128)}), f32[8,6,128]{2,1,0:T(8,128)S(1)}, u32[]{:S(2)}, u32[]{:S(2)}) async-start(f32[8,6,128]{2,1,0:T(8,128)} %reshape.289), calls=%async_computation.2 | async-start | bytes 65536 | tf_op jit(solution)/shard_map/all_to_all | solution.py:270
  38.8 8.3 %all-to-all-start.1 = ((f32[8,6,384]{2,1,0:T(8,128)}), f32[8,6,384]{2,1,0:T(8,128)S(1)}, u32[]{:S(2)}, u32[]{:S(2)}) async-start(f32[8,6,384]{2,1,0:T(8,128)} %fusion.23), calls=%async_computation.1 | async-start | bytes 196608 | tf_op jit(solution)/shard_map/all_to_all | solution.py:269
  42.8 102.6 %all-gather.4.cloned.1.call-start = ((), (), s32[]{:S(2)}) async-start(), calls=%async_computation.7 | async-start | bytes 2621440 | tf_op jit(solution)/shard_map/all_gather | solution.py:289
  48.7 53.2 %copy-start = (f32[8,16,128]{2,1,0:T(8,128)S(1)}, f32[8,16,128]{2,1,0:T(8,128)}, u32[]{:S(2)}) copy-start(f32[8,16,128]{2,1,0:T(8,128)} %param.7) | copy-start | bytes 196612
  115.4 11.1 %all-to-all-start.3 = ((f32[8,6,2048]{2,1,0:T(8,128)}), f32[8,6,2048]{2,1,0:T(8,128)S(1)}, u32[]{:S(2)}, u32[]{:S(2)}) async-start(f32[8,6,2048]{2,1,0:T(8,128)} %fusion.15), calls=%async_computation.3 | async-start | bytes 1048576 | tf_op jit(solution)/shard_map/all_to_all | solution.py:256
  204.8 6.1 %copy-start.1 = (u32[32]{0:T(128)S(1)}, u32[32]{0:T(128)}, u32[]{:S(2)}) copy-start(u32[32]{0:T(128)} %constant.61) | copy-start | bytes 388
  206.2 22.9 %all-to-all-start.6 = ((f32[8,6,2048]{2,1,0:T(8,128)}), f32[8,6,2048]{2,1,0:T(8,128)S(1)}, u32[]{:S(2)}, u32[]{:S(2)}) async-start(f32[8,6,2048]{2,1,0:T(8,128)} %fusion.17), calls=%async_computation.6 | async-start | bytes 1048576 | tf_op jit(solution)/shard_map/all_to_all | solution.py:263
Sparse Core Ops, SparseCore 0:
  102.0 43.3 all-gather.3
where the time goes:
time: 257 us; the launch traced here: 254 us
  blocking collectives  98.5 us (38%)
  Pallas kernels  50.9 us (20%)
  waiting for transfers between devices  35.1 us (14%)
  starting transfers between devices  22.1 us (9%)
  between operations  15.6 us (6%)
  local copies, waits for them, and re-layouts  14.3 us (6%)
  matrix products  13.4 us (5%)
  other arithmetic  4.13 us (2%)
    pallas_call x1, Pallas kernels, factor_blocks(): pl.pallas_call(factor_kernel, out_shape=(jax.ShapeDtypeStruct((nb, bs, or...  50.9 us
    all_gather x1, waiting for transfers between devices, body(): lax.all_gather(conditioner, 'probe', axis=0, tiled=True)  18.7 us
    psum x1, blocking collectives, body(): alpha_two = lax.psum(local_inner(basis_two, image_two), 'rows') / cells  15.6 us
    all_to_all x1, blocking collectives, return_terms(): lax.all_to_all(outgoing, 'rows', split_axis=0, concat_axis=0, tiled=True)  13.1 us
    psum x1, blocking collectives, body(): alpha_one = lax.psum(local_inner(basis_one, image_one), 'rows') / cells  12.4 us
    psum x1, blocking collectives, body(): square_sum = lax.psum(local_inner(probes, probes), 'rows')  12.1 us
    psum x1, blocking collectives, body(): lax.psum(local_inner(residue, residue), 'rows') / cells + epsilon  11.8 us
    all_to_all x1, blocking collectives, fetch_rows(): lax.all_to_all(select_rows(source), 'rows', split_axis=0, concat_axis=0,...  11.7 us
  transfers between devices with their start and end apart: 6, of which 5 were waited for; matrix products, arithmetic and copies ran while one was open for 3% of the time, Pallas kernels for 0%

commit v1 on v0

v1 whole, which is shorter than its diff:
```python
import functools
import math

import jax
import jax.numpy as jnp
from jax import lax
from jax.experimental import pallas as pl
from jax.experimental.pallas import tpu as pltpu
from jax.sharding import PartitionSpec as P

length_scale = 0.3
nugget = 0.25
epsilon = 1e-06
highest = lax.Precision.HIGHEST
chunk = 8
width = 4


def dot(left, right):
    return jnp.dot(left, right, precision=highest, preferred_element_type=jnp.float32)


def dot_nt(left, right):
    return lax.dot_general(
        left, right, (((1,), (1,)), ((), ())), precision=highest,
        preferred_element_type=jnp.float32,
    )


def pivot_inverse(rows, e):
    rows = list(rows)
    e = [list(r) for r in e]
    for k in range(width):
        inv = 1.0 / e[k][k]
        rows[k] = rows[k] * inv
        for n in range(k + 1, width):
            e[k][n] = e[k][n] * inv
        for m in range(width):
            if m != k:
                f = e[m][k]
                rows[m] = rows[m] - f * rows[k]
                for n in range(k + 1, width):
                    e[m][n] = e[m][n] - f * e[k][n]
    return rows


def pivot_factor(rows, e):
    e = [list(r) for r in e]
    y = list(rows)
    inv = []
    product = None
    for k in range(width):
        d = e[k][k]
        s = lax.rsqrt(d)
        s = s * (1.5 - 0.5 * d * s * s)
        inv.append(s)
        product = s if product is None else product * s
        y[k] = y[k] * s
        for m in range(k + 1, width):
            e[m][k] = e[m][k] * s
        for m in range(k + 1, width):
            y[m] = y[m] - e[m][k] * y[k]
            for n in range(k + 1, m + 1):
                e[m][n] = e[m][n] - e[m][k] * e[n][k]
    r = list(y)
    for k in reversed(range(width)):
        for m in range(k + 1, width):
            r[k] = r[k] - e[m][k] * r[m]
        r[k] = r[k] * inv[k]
    return y, r, jnp.log(product)


def sweep(mats, factor):
    count = len(mats[0])
    shape = mats[0][0].shape
    lane = lax.broadcasted_iota(jnp.int32, shape, 1)
    sub = lax.broadcasted_iota(jnp.int32, shape, 0)

    def full(x):
        return jnp.broadcast_to(x, shape)

    def step(t, carry):
        mats, logs = carry
        mats = [list(m) for m in mats]
        logs = list(logs)
        for o in range(0, chunk, width):
            picked = (lane >= o) & (lane < o + width)
            for b in range(len(mats)):
                chunks = mats[b]
                top = chunks[0]
                cols = [full(top[:, o + k : o + k + 1]) for k in range(width)]
                rows = [full(top[o + k : o + k + 1, :]) for k in range(width)]
                e = [[full(cols[k][o + m : o + m + 1, :]) for k in range(width)] for m in range(width)]
                rows = [
                    jnp.where(lane == o + k, 1.0, jnp.where(picked, 0.0, rows[k]))
                    for k in range(width)
                ]
                if factor:
                    kept, r, term = pivot_factor(rows, e)
                    logs[b] = logs[b] + term
                else:
                    r = pivot_inverse(rows, e)
                    kept = r
                for p in range(count):
                    old = chunks[p]
                    if p:
                        cols = [full(old[:, o + k : o + k + 1]) for k in range(width)]
                    new = jnp.where(picked, 0.0, old)
                    for k in range(width):
                        new = new - cols[k] * r[k]
                    if p == 0:
                        if factor:
                            new = jnp.where(sub >= o + width, new, old)
                        for k in range(width):
                            new = jnp.where(sub == o + k, kept[k], new)
                    elif factor:
                        new = jnp.where(t + p < count, new, old)
                    chunks[p] = new
        turned = []
        for chunks in mats:
            chunks = [pltpu.roll(c, shape[1] - chunk, 1) for c in chunks]
            turned.append(tuple(chunks[1:] + chunks[:1]))
        return tuple(turned), tuple(logs)

    zero = jnp.zeros(shape, jnp.float32)
    return lax.fori_loop(0, count, step, (mats, tuple(zero for _ in mats)))


MESH = pl.DeviceIdType.MESH


def to_peers(axis, count, source, target, send_sem, recv_sem):
    me = lax.axis_index(axis)
    copies = []
    for p in range(1, count):
        peer = lax.rem(me + p, count)
        copies.append(
            pltpu.make_async_remote_copy(
                src_ref=source(peer),
                dst_ref=target,
                send_sem=send_sem.at[p - 1],
                recv_sem=recv_sem.at[p - 1],
                device_id={axis: peer},
                device_id_type=MESH,
            )
        )
    for copy in copies:
        copy.start()
    return copies


def wait_all(copies):
    for copy in copies:
        copy.wait()


def greet(counts):
    barrier = pltpu.get_barrier_semaphore()
    total = 0
    for axis, count in counts:
        for p in range(1, count):
            peer = lax.rem(lax.axis_index(axis) + p, count)
            pl.semaphore_signal(barrier, inc=1, device_id={axis: peer}, device_id_type=MESH)
            total += 1
    pl.semaphore_wait(barrier, total)


def gather_kernel(count, *refs):
    half = 4
    sources, targets, (send_sem, recv_sem, own_sem) = refs[:half], refs[half : 2 * half], refs[2 * half :]
    me = lax.axis_index("rows")
    greet((("rows", count),))
    copies = []
    for i in range(half):
        copies += to_peers(
            "rows", count, lambda peer: sources[i], targets[i].at[me], send_sem.at[i], recv_sem.at[i]
        )
    owns = [
        pltpu.make_async_copy(sources[i], targets[i].at[me], own_sem.at[i]) for i in range(half)
    ]
    for own in owns:
        own.start()
    for own in owns:
        own.wait()
    wait_all(copies)


def gather_rows(count, arrays):
    vmem = pl.BlockSpec(memory_space=pltpu.VMEM)
    return pl.pallas_call(
        functools.partial(gather_kernel, count),
        out_shape=[jax.ShapeDtypeStruct((count,) + a.shape, a.dtype) for a in arrays],
        in_specs=[vmem] * len(arrays),
        out_specs=[vmem] * len(arrays),
        scratch_shapes=[
            pltpu.SemaphoreType.DMA((len(arrays), count - 1)),
            pltpu.SemaphoreType.DMA((len(arrays), count - 1)),
            pltpu.SemaphoreType.DMA((len(arrays),)),
        ],
        compiler_params=pltpu.CompilerParams(collective_id=0, has_side_effects=True),
    )(*arrays)


def factor_kernel(
    capacity, share, first_ref, near_ref, pos_ref, points_ref, values_ref,
    g_ref, slot_ref, recv_ref, a_ref, seen_ref,
):
    nb = g_ref.shape[0]
    bs = points_ref.shape[3]
    count, blocks = points_ref.shape[:2]
    me = first_ref[0]
    first = first_ref[1]

    def position(owner, b, j):
        ident = near_ref[owner, b, j]
        return pos_ref[ident // blocks, 0, ident % blocks]

    def clear(i, c):
        slot_ref[i] = 3 * blocks
        recv_ref[i] = -1
        return c

    lax.fori_loop(0, count * capacity, clear, 0)

    def clear_seen(i, c):
        seen_ref[i] = 0
        return c

    lax.fori_loop(0, 2 * count, clear_seen, 0)

    def place_own(b, c):
        for j in range(3):
            at = position(me, b, j) // blocks
            rank = seen_ref[at]
            seen_ref[at] = rank + 1
            slot_ref[at * capacity + rank] = b * 3 + j
        return c

    lax.fori_loop(0, blocks, place_own, 0)

    def place(i, c):
        for j in range(3):
            sender = i // blocks
            row = position(sender, i % blocks, j)

            @pl.when(row // blocks == me)
            def _():
                rank = seen_ref[count + sender]
                seen_ref[count + sender] = rank + 1
                recv_ref[sender * capacity + rank] = row % blocks

        return c

    lax.fori_loop(0, count * blocks, place, 0)

    def part(i):
        return slice(i * bs, (i + 1) * bs)

    def load(j):
        return tuple(
            tuple(
                a_ref[b, j * bs + i * chunk : j * bs + (i + 1) * chunk, part(j)]
                for i in range(bs // chunk)
            )
            for b in range(nb)
        )

    same = lax.broadcasted_iota(jnp.int32, (bs, bs), 0) == lax.broadcasted_iota(
        jnp.int32, (bs, bs), 1
    )
    below = lax.broadcasted_iota(jnp.int32, (bs, bs), 0) >= lax.broadcasted_iota(
        jnp.int32, (bs, bs), 1
    )
    values = []
    for b in range(nb):
        at = [(position(me, first + b, j)) for j in range(3)]
        at = [(row // blocks, row % blocks) for row in at] + [(me, first + b)]
        rows = [points_ref[o, r] for o, r in at]
        values.append(
            jnp.concatenate(
                [jnp.broadcast_to(values_ref[o, pl.ds(r, 1)], (chunk, bs)) for o, r in at], axis=1
            )
        )
        pad = jnp.zeros((chunk - rows[0].shape[0], bs), jnp.float32)
        cols = [jnp.transpose(jnp.concatenate([row, pad], axis=0)) for row in rows]
        for i in range(4):
            for k in range(i + 1):
                dist_sq = None
                for c in range(3):
                    off = cols[i][:, c : c + 1] - rows[k][c : c + 1, :]
                    dist_sq = off * off if dist_sq is None else dist_sq + off * off
                value = 1.0 / (1.0 + dist_sq * (1.0 / (length_scale * length_scale)))
                if i == k:
                    value = value + jnp.where(same, nugget, 0.0)
                a_ref[b, part(i), part(k)] = value
    for j in range(3):
        inverse, _ = sweep(load(j), False)
        for b in range(nb):
            p = jnp.concatenate(inverse[b], axis=0)
            rest = a_ref[b, (j + 1) * bs :, part(j)]
            scaled = dot(rest, p)
            for i in range(j + 1, 4):
                row = scaled[(i - j - 1) * bs : (i - j) * bs]
                a_ref[b, part(i), (j + 1) * bs : (i + 1) * bs] -= dot_nt(
                    row, rest[: (i - j) * bs]
                )
            a_ref[b, (j + 1) * bs :, part(j)] = scaled
    low, logs = sweep(load(3), True)
    for b in range(nb):
        low_inv = jnp.where(below, jnp.concatenate(low[b], axis=0), 0.0)
        x2 = a_ref[b, part(3), part(2)]
        x1 = a_ref[b, part(3), part(1)] - dot(x2, a_ref[b, part(2), part(1)])
        x0 = (
            a_ref[b, part(3), part(0)]
            - dot(x1, a_ref[b, part(1), part(0)])
            - dot(x2, a_ref[b, part(2), part(0)])
        )
        g_ref[b, :bs, part(3)] = low_inv
        for i, x in enumerate((x0, x1, x2)):
            g_ref[b, :bs, part(i)] = -dot(low_inv, x)
        w = dot_nt(values[b], g_ref[b, :bs])
        square = jnp.sum(w[:1] * w[:1], axis=1, keepdims=True)
        term = (logs[b] - 0.5 * square) * (1.0 / bs) - 0.5 * math.log(2.0 * math.pi)
        g_ref[b, bs:, :] = jnp.concatenate([w, term, w, term], axis=1)


def factor_blocks(first, near, positions, points, values, nb, capacity):
    count, blocks, _, bs = points.shape
    smem = pl.BlockSpec(memory_space=pltpu.SMEM)
    vmem = pl.BlockSpec(memory_space=pltpu.VMEM)
    slots = jax.ShapeDtypeStruct((count * capacity,), jnp.int32)
    return pl.pallas_call(
        functools.partial(factor_kernel, capacity, nb),
        out_shape=(jax.ShapeDtypeStruct((nb, bs + chunk, 4 * bs), jnp.float32), slots, slots),
        in_specs=[smem, smem, smem, vmem, vmem],
        out_specs=(vmem, smem, smem),
        scratch_shapes=[
            pltpu.VMEM((nb, 4 * bs, 4 * bs), jnp.float32),
            pltpu.SMEM((2 * count,), jnp.int32),
        ],
        cost_estimate=pl.CostEstimate(
            flops=10**10, bytes_accessed=10**6, transcendentals=0
        ),
    )(first, near, positions, points, values)


def lanczos_kernel(
    count, depth, capacity, near_ref, pos_ref, slot_ref, recv_ref, g_ref, probes_ref,
    rem_ref, tri_ref, w_ref, t_ref,
    gall, q, z, sp, own, sb1, sb2, rb1, rb2,
    g_send, g_recv, r1_send, r1_recv, z_send, z_recv, r2_send, r2_recv, own_sem,
):
    me = lax.axis_index("rows")
    level = lax.axis_index("probe")
    total, cols, bs = probes_ref.shape
    blocks = total // count
    nb = g_ref.shape[0]
    cells = total * bs
    greet((("rows", count), ("probe", depth)))
    mine = gall.at[pl.ds(level * nb, nb)]
    g_copies = to_peers("probe", depth, lambda peer: g_ref, mine, g_send, g_recv)
    keep = pltpu.make_async_copy(g_ref, mine, own_sem)
    keep.start()

    def inner(f):
        acc = jnp.zeros((cols, bs), jnp.float32)
        for c in range(total):
            acc = acc + f(c)
        return jnp.sum(acc, axis=1, keepdims=True)

    scale = 1.0 / jnp.sqrt(inner(lambda c: probes_ref[c] * probes_ref[c]) / cells + epsilon)
    for c in range(total):
        q[c] = probes_ref[c] * scale
    sp[3 * blocks] = jnp.zeros((cols, bs), jnp.float32)
    keep.wait()
    wait_all(g_copies)
    for b in range(blocks):
        w_ref[b : b + 1] = gall[b, bs : bs + 1, :bs]
        t_ref[b : b + 1] = gall[b, bs : bs + 1, bs : 2 * bs]

    def apply_operator(source, sb, rb, send_sem, recv_sem):
        energy = jnp.zeros((cols, bs), jnp.float32)
        for b in range(blocks):
            parts = []
            for j in range(3):
                ident = near_ref[b, j]
                parts.append(source[pos_ref[ident // blocks, 0, ident % blocks]])
            parts.append(source[me * blocks + b])
            g = gall[b, :bs]
            projected = dot_nt(jnp.concatenate(parts, axis=1), g)
            energy = energy + projected * projected
            spread = dot(projected, g)
            for j in range(3):
                sp[b * 3 + j] = spread[:, j * bs : (j + 1) * bs]
            own[b] = spread[:, 3 * bs :]
        for d in range(count):
            for k in range(capacity):
                sb[d, k] = sp[slot_ref[d * capacity + k]]
            sb[d, capacity] = energy
        copies = to_peers("rows", count, lambda peer: sb.at[peer], rb.at[me], send_sem, recv_sem)
        rb[me] = sb[me]
        wait_all(copies)
        sums = [own[b] for b in range(blocks)]
        energy = jnp.zeros((cols, bs), jnp.float32)
        for d in range(count):
            for k in range(capacity):
                value = rb[d, k]
                local = recv_ref[d * capacity + k]
                for b in range(blocks):
                    sums[b] = sums[b] + jnp.where(local == b, value, 0.0)
            energy = energy + rb[d, capacity]
        return sums, jnp.sum(energy, axis=1, keepdims=True) / cells

    image, alpha_one = apply_operator(q, sb1, rb1, r1_send, r1_recv)
    for b in range(blocks):
        z[me * blocks + b] = image[b]
    here = z.at[pl.ds(me * blocks, blocks)]
    wait_all(to_peers("rows", count, lambda peer: here, here, z_send, z_recv))

    def residue(c):
        r = z[c] - alpha_one * q[c]
        return r * r

    beta_one = jnp.sqrt(inner(residue) / cells + epsilon)
    over = 1.0 / beta_one
    for b in range(blocks):
        own_q = q[me * blocks + b]
        rem_ref[b] = own_q
    for c in range(total):
        q[c] = (z[c] - alpha_one * q[c]) * over
    image, alpha_two = apply_operator(q, sb2, rb2, r2_send, r2_recv)
    for b in range(blocks):
        rem_ref[b] = image[b] - alpha_two * q[me * blocks + b] - beta_one * rem_ref[b]
    lane = lax.broadcasted_iota(jnp.int32, (cols, bs), 1)
    tri_ref[...] = jnp.where(lane == 0, alpha_one, jnp.where(lane == 1, beta_one, alpha_two))


def lanczos(count, depth, capacity, near, positions, slots, received, g, probes):
    total, cols, bs = probes.shape
    blocks = total // count
    smem = pl.BlockSpec(memory_space=pltpu.SMEM)
    vmem = pl.BlockSpec(memory_space=pltpu.VMEM)
    f32 = jnp.float32
    dma = pltpu.SemaphoreType.DMA
    exchange = pltpu.VMEM((count, capacity + 1, cols, bs), f32)
    return pl.pallas_call(
        functools.partial(lanczos_kernel, count, depth, capacity),
        out_shape=(
            jax.ShapeDtypeStruct((blocks, cols, bs), f32),
            jax.ShapeDtypeStruct((cols, bs), f32),
            jax.ShapeDtypeStruct((blocks, bs), f32),
            jax.ShapeDtypeStruct((blocks, bs), f32),
        ),
        in_specs=[smem] * 4 + [vmem] * 2,
        out_specs=(vmem,) * 4,
        scratch_shapes=[
            pltpu.VMEM((blocks,) + g.shape[1:], f32),
            pltpu.VMEM((total, cols, bs), f32),
            pltpu.VMEM((total, cols, bs), f32),
            pltpu.VMEM((3 * blocks + 1, cols, bs), f32),
            pltpu.VMEM((blocks, cols, bs), f32),
            exchange, exchange, exchange, exchange,
        ]
        + [dma((depth - 1,))] * 2
        + [dma((count - 1,))] * 6
        + [dma],
        compiler_params=pltpu.CompilerParams(collective_id=1, has_side_effects=True),
    )(near, positions, slots, received, g, probes)


def body(points, observations, probes, neighbours, block_position):
    count = lax.axis_size("rows")
    depth = lax.axis_size("probe")
    blocks = points.shape[0]
    capacity = max(2, 6 * blocks // count)
    nb = blocks // depth
    points_all, values_all, near_all, positions = gather_rows(
        count, (points, observations, neighbours, block_position.reshape(1, blocks))
    )
    probes_all = lax.all_gather(probes, "rows", axis=0, tiled=True)
    first = jnp.stack([lax.axis_index("rows"), lax.axis_index("probe") * nb]).astype(jnp.int32)
    g, slots, received = factor_blocks(
        first, near_all, positions, points_all, values_all, nb, capacity
    )
    remainder, tri, whitened, terms = lanczos(
        count, depth, capacity, neighbours, positions, slots, received, g, probes_all
    )
    return (whitened, terms[:, 0], tri[:, :3], remainder)


def solution(mesh):
    placed = (
        P("rows", None, None),
        P("rows", None),
        P("rows", "probe", None),
        P("rows", None),
        P("rows"),
    )
    return jax.shard_map(
        body,
        mesh=mesh,
        in_specs=placed,
        out_specs=(P("rows", None), P("rows"), P("probe", None), P("rows", "probe", None)),
        check_vma=False,
    )
```

time: 257 us -> 169 us (0.66); the launches traced: 254 us -> 169 us
  Pallas kernels: 50.9 us -> 151 us
  blocking collectives: 98.5 us -> 11.3 us
  waiting for transfers between devices: 35.1 us -> 0 us
  starting transfers between devices: 22.1 us -> 0 us
  between operations: 15.6 us -> 0.7 us
  matrix products: 13.4 us -> 0 us
  local copies, waits for them, and re-layouts: 14.3 us -> 5.42 us
  other arithmetic: 4.13 us -> 0.61 us
    pallas_call x1 -> x3, Pallas kernels: 50.9 us -> 151 us  [the longest x1 86.8 us: lanczos(): pl.pallas_call(functools.partial(lanczos_kernel, count, depth, capacity),...]
    psum x4 -> x0, blocking collectives: 51.9 us -> none  [the longest x1 15.6 us: body(): alpha_two = lax.psum(local_inner(basis_two, image_two), 'rows') / cells]
    all_to_all x2 -> x0, blocking collectives: 24.8 us -> none  [the longest x1 13.1 us: return_terms(): lax.all_to_all(outgoing, 'rows', split_axis=0, concat_axis=0, tiled=True)]
    all_to_all x5 -> x0, starting transfers between devices: 22.1 us -> none  [the longest x1 5.43 us: body(): lax.all_to_all(wanted.reshape(row_count, capacity), 'rows', split_axis=0,...]
    all_gather x1 -> x0, waiting for transfers between devices: 18.7 us -> none  [body(): lax.all_gather(conditioner, 'probe', axis=0, tiled=True)]
    all_to_all x5 -> x0, waiting for transfers between devices: 16.5 us -> none  [the longest x1 6.81 us: fetch_rows(): lax.all_to_all(select_rows(source), 'rows', split_axis=0, concat_axis=0,...]
    dot_general x16 -> x0, matrix products: 13.4 us -> none  [the longest x4 3.97 us: select_rows(): jnp.dot(picked, source, precision=highest)]
    unnamed x1 -> x0, blocking collectives: 6.47 us -> none
  transfers between devices with their start and end apart: 6 -> 0, of which waited for: 5 -> 0; matrix products, arithmetic and copies ran while one was open for 3% -> 0% of each run, Pallas kernels for 0% -> 0%
where the time goes in v1:
time: 169 us
  Pallas kernels  151 us (89%)
  blocking collectives  11.3 us (7%)
  local copies, waits for them, and re-layouts  5.42 us (3%)
    pallas_call x1, Pallas kernels, lanczos(): pl.pallas_call(functools.partial(lanczos_kernel, count, depth, capacity),...  86.8 us
    pallas_call x1, Pallas kernels, factor_blocks(): pl.pallas_call(functools.partial(factor_kernel, capacity, nb), out_shape=...  56 us
    all_gather x1, blocking collectives, body(): probes_all = lax.all_gather(probes, 'rows', axis=0, tiled=True)  11.3 us
    pallas_call x1, Pallas kernels, gather_rows(): pl.pallas_call(functools.partial(gather_kernel, count), out_shape=[jax.Sh...  7.99 us
    unnamed x15, local copies, waits for them, and re-layouts  4.1 us

profile of v1, /device:TPU:9, one launch (start us, length us, event | category | flops | bytes accessed | tf_op | source)
XLA Modules:
  0.0 168.8 jit_solution(17689801946873432348)
XLA Ops:
  0.6 0.0 copy-start.1
  0.6 0.0 copy-start.4
  0.7 0.6 pad_add_fusion.first_ref
  1.3 0.1 copy-done.4
  1.3 0.7 copy.19.refs_2_.near_ref
  2.0 0.0 copy-done.1
  2.0 0.6 copy.17.refs_0_
  2.6 8.0 %shard_map.84 = (f32[8,8,3,128]{3,2,1,0:T(4,128)}, f32[8,8,128]{2,1,0:T(8,128)}, s32[8,8,3]{2,1,0:T(8,128)}, s32[8,1,8]{2,1,0:T(1,128)}) custom-call(f32[8,3,128]{2,1,0:T(4,128)} %copy.17.refs_0_, f32[8,128]{1,0:T(8,128)} %refs_1_.1, s32[8,3]{1,0:T(8,128)} %copy.19.refs_2_.near_ref, s32[1,8]{1,0:T(1,128)} %bitcast.5), custom_call_target="tpu_custom_call" | custom-call | tf_op jit(solution)/shard_map/pallas_call | solution.py:190
  10.6 0.0 copy-start
  10.6 56.0 %shard_map.85 = (f32[2,136,512]{2,1,0:T(8,128)}, s32[48]{0:T(128)}, s32[48]{0:T(128)}) custom-call(s32[2]{0:T(128)} %pad_add_fusion.first_ref, s32[8,8,3]{2,1,0:T(8,128)} %get-tuple-element.16.near_ref, s32[8,1,8]{2,1,0:T(1,128)} %get-tuple-element.15.pos_ref, f32[8,8,3,128]{3,2,1,0:T(4,128)} %get-tuple-element.17.points_ref, ...), custom_call_target="tpu_custom_call" | custom-call | flops 10000000000 | bytes 1000000 | tf_op jit(solution)/shard_map/pallas_call | solution.py:332
  66.7 0.0 copy-done
  66.7 11.3 %all_gather.3.probes_ref = f32[64,16,128]{2,1,0:T(8,128)} all-gather(f32[8,16,128]{2,1,0:T(8,128)S(1)} %copy-done), channel_id=1, replica_groups=mesh['rows'=8,'probe'=4] {'rows'}, dimensions={0}, use_global_device_ids=true | all-gather | bytes 589824 | tf_op jit(solution)/shard_map/all_gather | solution.py:480
  78.0 86.8 %shard_map.86 = (f32[8,16,128]{2,1,0:T(8,128)}, f32[16,128]{1,0:T(8,128)}, f32[8,128]{1,0:T(8,128)}, f32[8,128]{1,0:T(8,128)}) custom-call(s32[8,3]{1,0:T(8,128)} %copy.19.refs_2_.near_ref, s32[8,1,8]{2,1,0:T(1,128)} %get-tuple-element.15.pos_ref, s32[48]{0:T(128)} %get-tuple-element.19.slot_ref, s32[48]{0:T(128)} %get-tuple-element.20.recv_ref, ...), custom_call_target="tpu_custom_call" | custom-call | tf_op jit(solution)/shard_map/pallas_call | solution.py:446
  164.8 0.0 copy-start.2
  164.8 1.3 slice_reduce_fusion
  166.1 0.0 copy-done.2
  166.1 0.0 copy-start.3
  166.1 0.7 copy.20
  166.8 0.0 copy-done.3
  166.8 0.6 copy.23
  167.4 1.5 copy.24
Async XLA Ops:
  0.6 1.4 copy-start.1
  0.6 0.7 copy-start.4
  10.6 56.0 %copy-start = (f32[8,16,128]{2,1,0:T(8,128)S(1)}, f32[8,16,128]{2,1,0:T(8,128)}, u32[]{:S(2)}) copy-start(f32[8,16,128]{2,1,0:T(8,128)} %param.7) | copy-start | bytes 196612
  164.8 1.3 copy-start.2
  166.1 0.7 copy-start.3

commit v2 on v1

--- a/solution.py
+++ b/solution.py
@@ -201,32 +201,19 @@
     )(*arrays)
 
 
-def factor_kernel(
-    capacity, share, first_ref, near_ref, pos_ref, points_ref, values_ref,
-    g_ref, slot_ref, recv_ref, a_ref, seen_ref,
-):
-    nb = g_ref.shape[0]
-    bs = points_ref.shape[3]
-    count, blocks = points_ref.shape[:2]
+def plan_kernel(capacity, first_ref, near_ref, pos_ref, slot_ref, recv_ref, seen_ref):
+    count, blocks = near_ref.shape[:2]
     me = first_ref[0]
-    first = first_ref[1]
 
     def position(owner, b, j):
         ident = near_ref[owner, b, j]
         return pos_ref[ident // blocks, 0, ident % blocks]
 
-    def clear(i, c):
+    for i in range(count * capacity):
         slot_ref[i] = 3 * blocks
         recv_ref[i] = -1
-        return c
-
-    lax.fori_loop(0, count * capacity, clear, 0)
-
-    def clear_seen(i, c):
+    for i in range(2 * count):
         seen_ref[i] = 0
-        return c
-
-    lax.fori_loop(0, 2 * count, clear_seen, 0)
 
     def place_own(b, c):
         for j in range(3):
@@ -253,34 +240,33 @@
 
     lax.fori_loop(0, count * blocks, place, 0)
 
+
+def plan_slots(first, near, positions, capacity):
+    count = near.shape[0]
+    smem = pl.BlockSpec(memory_space=pltpu.SMEM)
+    slots = jax.ShapeDtypeStruct((count * capacity,), jnp.int32)
+    return pl.pallas_call(
+        functools.partial(plan_kernel, capacity),
+        out_shape=(slots, slots),
+        in_specs=[smem] * 3,
+        out_specs=(smem, smem),
+        scratch_shapes=[pltpu.SMEM((2 * count,), jnp.int32)],
+    )(first, near, positions)
+
+
+def build_kernels(near_rows, me, first, points_ref, a_ref):
+    nb = a_ref.shape[0]
+    blocks, _, bs = points_ref.shape[1:]
+
     def part(i):
         return slice(i * bs, (i + 1) * bs)
 
-    def load(j):
-        return tuple(
-            tuple(
-                a_ref[b, j * bs + i * chunk : j * bs + (i + 1) * chunk, part(j)]
-                for i in range(bs // chunk)
-            )
-            for b in range(nb)
-        )
-
     same = lax.broadcasted_iota(jnp.int32, (bs, bs), 0) == lax.broadcasted_iota(
         jnp.int32, (bs, bs), 1
     )
-    below = lax.broadcasted_iota(jnp.int32, (bs, bs), 0) >= lax.broadcasted_iota(
-        jnp.int32, (bs, bs), 1
-    )
-    values = []
     for b in range(nb):
-        at = [(position(me, first + b, j)) for j in range(3)]
-        at = [(row // blocks, row % blocks) for row in at] + [(me, first + b)]
+        at = [(row // blocks, row % blocks) for row in near_rows[b]] + [(me, first + b)]
         rows = [points_ref[o, r] for o, r in at]
-        values.append(
-            jnp.concatenate(
-                [jnp.broadcast_to(values_ref[o, pl.ds(r, 1)], (chunk, bs)) for o, r in at], axis=1
-            )
-        )
         pad = jnp.zeros((chunk - rows[0].shape[0], bs), jnp.float32)
         cols = [jnp.transpose(jnp.concatenate([row, pad], axis=0)) for row in rows]
         for i in range(4):
@@ -293,6 +279,27 @@
                 if i == k:
                     value = value + jnp.where(same, nugget, 0.0)
                 a_ref[b, part(i), part(k)] = value
+
+
+def factor_blocks(near_rows, me, first, values_ref, a_ref, g_ref, wt_ref):
+    nb, bs = g_ref.shape[:2]
+    blocks = values_ref.shape[1]
+
+    def part(i):
+        return slice(i * bs, (i + 1) * bs)
+
+    def load(j):
+        return tuple(
+            tuple(
+                a_ref[b, j * bs + i * chunk : j * bs + (i + 1) * chunk, part(j)]
+                for i in range(bs // chunk)
+            )
+            for b in range(nb)
+        )
+
+    below = lax.broadcasted_iota(jnp.int32, (bs, bs), 0) >= lax.broadcasted_iota(
+        jnp.int32, (bs, bs), 1
+    )
     for j in range(3):
         inverse, _ = sweep(load(j), False)
         for b in range(nb):
@@ -315,52 +322,53 @@
             - dot(x1, a_ref[b, part(1), part(0)])
             - dot(x2, a_ref[b, part(2), part(0)])
         )
-        g_ref[b, :bs, part(3)] = low_inv
+        g_ref[b, :, part(3)] = low_inv
         for i, x in enumerate((x0, x1, x2)):
-            g_ref[b, :bs, part(i)] = -dot(low_inv, x)
-        w = dot_nt(values[b], g_ref[b, :bs])
+            g_ref[b, :, part(i)] = -dot(low_inv, x)
+        at = [(row // blocks, row % blocks) for row in near_rows[b]] + [(me, first + b)]
+        values = jnp.concatenate(
+            [jnp.broadcast_to(values_ref[o, pl.ds(r, 1)], (chunk, bs)) for o, r in at], axis=1
+        )
+        w = dot_nt(values, g_ref[b])
         square = jnp.sum(w[:1] * w[:1], axis=1, keepdims=True)
         term = (logs[b] - 0.5 * square) * (1.0 / bs) - 0.5 * math.log(2.0 * math.pi)
-        g_ref[b, bs:, :] = jnp.concatenate([w, term, w, term], axis=1)
-
-
-def factor_blocks(first, near, positions, points, values, nb, capacity):
-    count, blocks, _, bs = points.shape
-    smem = pl.BlockSpec(memory_space=pltpu.SMEM)
-    vmem = pl.BlockSpec(memory_space=pltpu.VMEM)
-    slots = jax.ShapeDtypeStruct((count * capacity,), jnp.int32)
-    return pl.pallas_call(
-        functools.partial(factor_kernel, capacity, nb),
-        out_shape=(jax.ShapeDtypeStruct((nb, bs + chunk, 4 * bs), jnp.float32), slots, slots),
-        in_specs=[smem, smem, smem, vmem, vmem],
-        out_specs=(vmem, smem, smem),
-        scratch_shapes=[
-            pltpu.VMEM((nb, 4 * bs, 4 * bs), jnp.float32),
-            pltpu.SMEM((2 * count,), jnp.int32),
-        ],
-        cost_estimate=pl.CostEstimate(
-            flops=10**10, bytes_accessed=10**6, transcendentals=0
-        ),
-    )(first, near, positions, points, values)
-
-
-def lanczos_kernel(
-    count, depth, capacity, near_ref, pos_ref, slot_ref, recv_ref, g_ref, probes_ref,
+        wt_ref[b] = jnp.concatenate([w, term], axis=1)
+
+
+def main_kernel(
+    count, depth, capacity,
+    near_ref, pos_ref, slot_ref, recv_ref, points_ref, values_ref, probes_ref,
     rem_ref, tri_ref, w_ref, t_ref,
-    gall, q, z, sp, own, sb1, sb2, rb1, rb2,
-    g_send, g_recv, r1_send, r1_recv, z_send, z_recv, r2_send, r2_recv, own_sem,
+    a_ref, g_ref, wt_all, probes_all, q, z, sp,
+    in1s, in1r, in2s, in2r, out1s, out1r, out2s, out2r, e1s, e1r, e2s, e2r,
+    sb1, sb2, rb1, rb2, zsem, rsem, own_sem,
 ):
     me = lax.axis_index("rows")
     level = lax.axis_index("probe")
-    total, cols, bs = probes_ref.shape
-    blocks = total // count
+    blocks, cols, bs = probes_ref.shape
+    total = blocks * count
     nb = g_ref.shape[0]
     cells = total * bs
+
+    def position(b, j):
+        ident = near_ref[me, b, j]
+        return pos_ref[ident // blocks, 0, ident % blocks]
+
+    def over_rows(i, source, target):
+        return to_peers("rows", count, source, target, rsem.at[2 * i], rsem.at[2 * i + 1])
+
+    def over_probe(i, source, target):
+        return to_peers("probe", depth, source, target, zsem.at[2 * i], zsem.at[2 * i + 1])
+
     greet((("rows", count), ("probe", depth)))
-    mine = gall.at[pl.ds(level * nb, nb)]
-    g_copies = to_peers("probe", depth, lambda peer: g_ref, mine, g_send, g_recv)
-    keep = pltpu.make_async_copy(g_ref, mine, own_sem)
+    here = pl.ds(me * blocks, blocks)
+    probe_copies = over_rows(0, lambda peer: probes_ref, probes_all.at[here])
+    keep = pltpu.make_async_copy(probes_ref, probes_all.at[here], own_sem)
     keep.start()
+
+    first = level * nb
+    near_rows = [[position(first + b, j) for j in range(3)] for b in range(nb)]
+    build_kernels(near_rows, me, first, points_ref, a_ref)
 
     def inner(f):
         acc = jnp.zeros((cols, bs), jnp.float32)
@@ -368,39 +376,54 @@
             acc = acc + f(c)
         return jnp.sum(acc, axis=1, keepdims=True)
 
-    scale = 1.0 / jnp.sqrt(inner(lambda c: probes_ref[c] * probes_ref[c]) / cells + epsilon)
+    def send_in(i, source, s, r):
+        for b in range(blocks):
+            parts = [source[position(b, j)] for j in range(3)] + [source[me * blocks + b]]
+            s[b // nb, b % nb] = jnp.concatenate(parts, axis=1)
+        copies = over_probe(i, lambda peer: s.at[peer], r.at[level])
+        r[level] = s[level]
+        return copies
+
+    keep.wait()
+    wait_all(probe_copies)
+    scale = 1.0 / jnp.sqrt(inner(lambda c: probes_all[c] * probes_all[c]) / cells + epsilon)
     for c in range(total):
-        q[c] = probes_ref[c] * scale
+        q[c] = probes_all[c] * scale
+    in_copies = send_in(0, q, in1s, in1r)
     sp[3 * blocks] = jnp.zeros((cols, bs), jnp.float32)
-    keep.wait()
-    wait_all(g_copies)
-    for b in range(blocks):
-        w_ref[b : b + 1] = gall[b, bs : bs + 1, :bs]
-        t_ref[b : b + 1] = gall[b, bs : bs + 1, bs : 2 * bs]
-
-    def apply_operator(source, sb, rb, send_sem, recv_sem):
-        energy = jnp.zeros((cols, bs), jnp.float32)
+    factor_blocks(near_rows, me, first, values_ref, a_ref, g_ref, wt_all.at[level])
+    wt_copies = over_probe(1, lambda peer: wt_all.at[level], wt_all.at[level])
+
+    def apply_operator(i, inr, outs, outr, es, er, sb, rb):
+        energy = jnp.zeros((depth * cols, bs), jnp.float32)
+        for b in range(nb):
+            stacked = jnp.concatenate([inr[d, b] for d in range(depth)], axis=0)
+            projected = dot_nt(stacked, g_ref[b])
+            energy = energy + projected * projected
+            spread = dot(projected, g_ref[b])
+            for d in range(depth):
+                outs[d, b] = spread[d * cols : (d + 1) * cols]
+        for d in range(depth):
+            es[d] = energy[d * cols : (d + 1) * cols]
+        copies = over_probe(2 * i, lambda peer: outs.at[peer], outr.at[level])
+        copies += over_probe(2 * i + 1, lambda peer: es.at[peer], er.at[level])
+        outr[level] = outs[level]
+        er[level] = es[level]
+        wait_all(copies)
+        energy = er[0]
+        for d in range(1, depth):
+            energy = energy + er[d]
         for b in range(blocks):
-            parts = []
             for j in range(3):
-                ident = near_ref[b, j]
-                parts.append(source[pos_ref[ident // blocks, 0, ident % blocks]])
-            parts.append(source[me * blocks + b])
-            g = gall[b, :bs]
-            projected = dot_nt(jnp.concatenate(parts, axis=1), g)
-            energy = energy + projected * projected
-            spread = dot(projected, g)
-            for j in range(3):
-                sp[b * 3 + j] = spread[:, j * bs : (j + 1) * bs]
-            own[b] = spread[:, 3 * bs :]
+                sp[b * 3 + j] = outr[b // nb, b % nb, :, j * bs : (j + 1) * bs]
         for d in range(count):
             for k in range(capacity):
                 sb[d, k] = sp[slot_ref[d * capacity + k]]
             sb[d, capacity] = energy
-        copies = to_peers("rows", count, lambda peer: sb.at[peer], rb.at[me], send_sem, recv_sem)
+        copies = over_rows(i, lambda peer: sb.at[peer], rb.at[me])
         rb[me] = sb[me]
         wait_all(copies)
-        sums = [own[b] for b in range(blocks)]
+        sums = [outr[b // nb, b % nb, :, 3 * bs :] for b in range(blocks)]
         energy = jnp.zeros((cols, bs), jnp.float32)
         for d in range(count):
             for k in range(capacity):
@@ -411,11 +434,11 @@
             energy = energy + rb[d, capacity]
         return sums, jnp.sum(energy, axis=1, keepdims=True) / cells
 
-    image, alpha_one = apply_operator(q, sb1, rb1, r1_send, r1_recv)
+    wait_all(in_copies)
+    image, alpha_one = apply_operator(1, in1r, out1s, out1r, e1s, e1r, sb1, rb1)
     for b in range(blocks):
         z[me * blocks + b] = image[b]
-    here = z.at[pl.ds(me * blocks, blocks)]
-    wait_all(to_peers("rows", count, lambda peer: here, here, z_send, z_recv))
+    wait_all(over_rows(2, lambda peer: z.at[here], z.at[here]))
 
     def residue(c):
         r = z[c] - alpha_one * q[c]
@@ -424,48 +447,57 @@
     beta_one = jnp.sqrt(inner(residue) / cells + epsilon)
     over = 1.0 / beta_one
     for b in range(blocks):
-        own_q = q[me * blocks + b]
-        rem_ref[b] = own_q
+        rem_ref[b] = q[me * blocks + b]
     for c in range(total):
         q[c] = (z[c] - alpha_one * q[c]) * over
-    image, alpha_two = apply_operator(q, sb2, rb2, r2_send, r2_recv)
+    wait_all(send_in(4, q, in2s, in2r))
+    image, alpha_two = apply_operator(3, in2r, out2s, out2r, e2s, e2r, sb2, rb2)
     for b in range(blocks):
         rem_ref[b] = image[b] - alpha_two * q[me * blocks + b] - beta_one * rem_ref[b]
     lane = lax.broadcasted_iota(jnp.int32, (cols, bs), 1)
     tri_ref[...] = jnp.where(lane == 0, alpha_one, jnp.where(lane == 1, beta_one, alpha_two))
-
-
-def lanczos(count, depth, capacity, near, positions, slots, received, g, probes):
-    total, cols, bs = probes.shape
-    blocks = total // count
+    wait_all(wt_copies)
+    for b in range(blocks):
+        w_ref[b : b + 1] = wt_all[b // nb, b % nb, :1, :bs]
+        t_ref[b : b + 1] = wt_all[b // nb, b % nb, :1, bs:]
+
+
+def main_call(count, depth, capacity, near, positions, slots, received, points, values, probes):
+    blocks, cols, bs = probes.shape
+    total = blocks * count
+    nb = blocks // depth
     smem = pl.BlockSpec(memory_space=pltpu.SMEM)
     vmem = pl.BlockSpec(memory_space=pltpu.VMEM)
     f32 = jnp.float32
     dma = pltpu.SemaphoreType.DMA
+    wide = pltpu.VMEM((depth, nb, cols, 4 * bs), f32)
+    small = pltpu.VMEM((depth, cols, bs), f32)
     exchange = pltpu.VMEM((count, capacity + 1, cols, bs), f32)
     return pl.pallas_call(
-        functools.partial(lanczos_kernel, count, depth, capacity),
+        functools.partial(main_kernel, count, depth, capacity),
         out_shape=(
             jax.ShapeDtypeStruct((blocks, cols, bs), f32),
             jax.ShapeDtypeStruct((cols, bs), f32),
             jax.ShapeDtypeStruct((blocks, bs), f32),
             jax.ShapeDtypeStruct((blocks, bs), f32),
         ),
-        in_specs=[smem] * 4 + [vmem] * 2,
+        in_specs=[smem] * 4 + [vmem] * 3,
         out_specs=(vmem,) * 4,
         scratch_shapes=[
-            pltpu.VMEM((blocks,) + g.shape[1:], f32),
+            pltpu.VMEM((nb, 4 * bs, 4 * bs), f32),
+            pltpu.VMEM((nb, bs, 4 * bs), f32),
+            pltpu.VMEM((depth, nb, chunk, 2 * bs), f32),
+            pltpu.VMEM((total, cols, bs), f32),
             pltpu.VMEM((total, cols, bs), f32),
             pltpu.VMEM((total, cols, bs), f32),
             pltpu.VMEM((3 * blocks + 1, cols, bs), f32),
-            pltpu.VMEM((blocks, cols, bs), f32),
-            exchange, exchange, exchange, exchange,
         ]
-        + [dma((depth - 1,))] * 2
-        + [dma((count - 1,))] * 6
-        + [dma],
+        + [wide] * 8
+        + [small] * 4
+        + [exchange] * 4
+        + [dma((16, depth - 1)), dma((8, count - 1)), dma],
         compiler_params=pltpu.CompilerParams(collective_id=1, has_side_effects=True),
-    )(near, positions, slots, received, g, probes)
+    )(near, positions, slots, received, points, values, probes)
 
 
 def body(points, observations, probes, neighbours, block_position):
@@ -473,17 +505,14 @@
     depth = lax.axis_size("probe")
     blocks = points.shape[0]
     capacity = max(2, 6 * blocks // count)
-    nb = blocks // depth
     points_all, values_all, near_all, positions = gather_rows(
         count, (points, observations, neighbours, block_position.reshape(1, blocks))
     )
-    probes_all = lax.all_gather(probes, "rows", axis=0, tiled=True)
-    first = jnp.stack([lax.axis_index("rows"), lax.axis_index("probe") * nb]).astype(jnp.int32)
-    g, slots, received = factor_blocks(
-        first, near_all, positions, points_all, values_all, nb, capacity
-    )
-    remainder, tri, whitened, terms = lanczos(
-        count, depth, capacity, neighbours, positions, slots, received, g, probes_all
+    first = lax.axis_index("rows").astype(jnp.int32).reshape(1)
+    slots, received = plan_slots(first, near_all, positions, capacity)
+    remainder, tri, whitened, terms = main_call(
+        count, depth, capacity, near_all, positions, slots, received,
+        points_all, values_all, probes,
     )
     return (whitened, terms[:, 0], tri[:, :3], remainder)
 

time: 169 us -> 133 us (0.79); the launches traced: 169 us -> 130 us
  Pallas kernels: 151 us -> 124 us
  blocking collectives: 11.3 us -> 0 us
    pallas_call x2, Pallas kernels: 143 us -> 116 us  [the longest x1 109 us: main_call(): pl.pallas_call(functools.partial(main_kernel, count, depth, capacity), ou...]
    all_gather x1 -> x0, blocking collectives: 11.3 us -> none  [body(): probes_all = lax.all_gather(probes, 'rows', axis=0, tiled=True)]
    unnamed x15 -> x11, local copies, waits for them, and re-layouts: 4.1 us -> 4.7 us
where the time goes in v2:
time: 133 us; the launch traced here: 130 us
  Pallas kernels  124 us (93%)
  local copies, waits for them, and re-layouts  6.01 us (5%)
    pallas_call x1, Pallas kernels, main_call(): pl.pallas_call(functools.partial(main_kernel, count, depth, capacity), ou...  109 us
    pallas_call x1, Pallas kernels, gather_rows(): pl.pallas_call(functools.partial(gather_kernel, count), out_shape=[jax.Sh...  7.98 us
    pallas_call x1, Pallas kernels, plan_slots(): pl.pallas_call(functools.partial(plan_kernel, capacity), out_shape=(slots...  6.26 us
    unnamed x11, local copies, waits for them, and re-layouts  4.7 us

profile of v2, /device:TPU:9, one launch (start us, length us, event | category | flops | bytes accessed | tf_op | source)
XLA Modules:
  0.0 130.4 jit_solution(13431578853536327741)
XLA Ops:
  0.6 0.0 copy-start
  0.6 1.3 %copy.13.refs_2_ = s32[8,3]{1,0:T(8,128)} copy(s32[8,3]{0,1:T(4,128)} %param.8) | data formatting | bytes 192 | tf_op args[3]
  2.0 0.0 copy-done
  2.0 0.6 copy.12.refs_0_
  2.6 8.0 %shard_map.84 = (f32[8,8,3,128]{3,2,1,0:T(4,128)}, f32[8,8,128]{2,1,0:T(8,128)}, s32[8,8,3]{2,1,0:T(8,128)}, s32[8,1,8]{2,1,0:T(1,128)}) custom-call(f32[8,3,128]{2,1,0:T(4,128)} %copy.12.refs_0_, f32[8,128]{1,0:T(8,128)} %refs_1_.1, s32[8,3]{1,0:T(8,128)} %copy.13.refs_2_, s32[1,8]{1,0:T(1,128)} %bitcast.4), custom_call_target="tpu_custom_call" | custom-call | tf_op jit(solution)/shard_map/pallas_call | solution.py:190
  10.6 6.3 %shard_map.85 = (s32[48]{0:T(128)}, s32[48]{0:T(128)}) custom-call(s32[1]{0:T(128)} %bitcast.1.first_ref, s32[8,8,3]{2,1,0:T(8,128)} %get-tuple-element.14.near_ref, s32[8,1,8]{2,1,0:T(1,128)} %get-tuple-element.15.pos_ref), custom_call_target="tpu_custom_call" | custom-call | tf_op jit(solution)/shard_map/pallas_call | solution.py:248
  16.9 109.5 %shard_map.86 = (f32[8,16,128]{2,1,0:T(8,128)}, f32[16,128]{1,0:T(8,128)}, f32[8,128]{1,0:T(8,128)}, f32[8,128]{1,0:T(8,128)}) custom-call(s32[8,8,3]{2,1,0:T(8,128)} %get-tuple-element.14.near_ref, s32[8,1,8]{2,1,0:T(1,128)} %get-tuple-element.15.pos_ref, s32[48]{0:T(128)} %get-tuple-element.16.slot_ref, s32[48]{0:T(128)} %get-tuple-element.17.recv_ref, ...), custom_call_target="tpu_custom_call" | custom-call | tf_op jit(solution)/shard_map/pallas_call | solution.py:476
  126.3 0.0 copy-start.1
  126.4 1.3 %slice_reduce_fusion = f32[8]{0:T(128)} fusion(f32[8,128]{1,0:T(8,128)} %get-tuple-element.21), kind=kLoop, calls=%fused_computation | loop fusion | bytes 64 | tf_op jit(solution)/shard_map/slice | solution.py:517
  127.7 0.0 copy-done.1
  127.7 0.0 copy-start.2
  127.7 0.7 copy.14
  128.3 0.0 copy-done.2
  128.3 0.6 copy.17
  128.9 1.5 %copy.18 = f32[8,16,128]{2,1,0:T(8,128)} copy(f32[8,16,128]{2,1,0:T(8,128)} %get-tuple-element.39) | data formatting | bytes 131072
Async XLA Ops:
  0.6 1.4 %copy-start = (f32[8,3,128]{2,0,1:T(8,128)S(1)}, f32[8,3,128]{2,0,1:T(8,128)}, u32[]{:S(2)}) copy-start(f32[8,3,128]{2,0,1:T(8,128)} %param.5) | copy-start | bytes 36868
  126.3 1.3 %copy-start.1 = (f32[16,128]{1,0:T(8,128)S(1)}, f32[16,128]{1,0:T(8,128)}, u32[]{:S(2)}) copy-start(f32[16,128]{1,0:T(8,128)} %get-tuple-element.22) | copy-start | bytes 24580
  127.7 0.7 copy-start.2

commit v3 on v2

--- a/solution.py
+++ b/solution.py
@@ -25,23 +25,6 @@
         left, right, (((1,), (1,)), ((), ())), precision=highest,
         preferred_element_type=jnp.float32,
     )
-
-
-def pivot_inverse(rows, e):
-    rows = list(rows)
-    e = [list(r) for r in e]
-    for k in range(width):
-        inv = 1.0 / e[k][k]
-        rows[k] = rows[k] * inv
-        for n in range(k + 1, width):
-            e[k][n] = e[k][n] * inv
-        for m in range(width):
-            if m != k:
-                f = e[m][k]
-                rows[m] = rows[m] - f * rows[k]
-                for n in range(k + 1, width):
-                    e[m][n] = e[m][n] - f * e[k][n]
-    return rows
 
 
 def pivot_factor(rows, e):
@@ -70,16 +53,17 @@
     return y, r, jnp.log(product)
 
 
-def sweep(mats, factor):
+def sweep(mats):
     count = len(mats[0])
     shape = mats[0][0].shape
     lane = lax.broadcasted_iota(jnp.int32, shape, 1)
     sub = lax.broadcasted_iota(jnp.int32, shape, 0)
+    segment = max(1, count // 4)
 
     def full(x):
         return jnp.broadcast_to(x, shape)
 
-    def step(t, carry):
+    def step(start, t, carry):
         mats, logs = carry
         mats = [list(m) for m in mats]
         logs = list(logs)
@@ -95,25 +79,23 @@
                     jnp.where(lane == o + k, 1.0, jnp.where(picked, 0.0, rows[k]))
                     for k in range(width)
                 ]
-                if factor:
-                    kept, r, term = pivot_factor(rows, e)
-                    logs[b] = logs[b] + term
-                else:
-                    r = pivot_inverse(rows, e)
-                    kept = r
-                for p in range(count):
+                kept, r, term = pivot_factor(rows, e)
+                logs[b] = logs[b] + term
+                for p in range(count - start):
                     old = chunks[p]
-                    if p:
-                        cols = [full(old[:, o + k : o + k + 1]) for k in range(width)]
-                    new = jnp.where(picked, 0.0, old)
-                    for k in range(width):
-                        new = new - cols[k] * r[k]
+                    if p == 0 and o + width == chunk:
+                        new = old
+                    else:
+                        if p:
+                            cols = [full(old[:, o + k : o + k + 1]) for k in range(width)]
+                        new = jnp.where(picked, 0.0, old)
+                        for k in range(width):
+                            new = new - cols[k] * r[k]
                     if p == 0:
-                        if factor:
-                            new = jnp.where(sub >= o + width, new, old)
+                        new = jnp.where(sub >= o + width, new, old)
                         for k in range(width):
                             new = jnp.where(sub == o + k, kept[k], new)
-                    elif factor:
+                    elif p > count - start - segment:
                         new = jnp.where(t + p < count, new, old)
                     chunks[p] = new
         turned = []
@@ -123,7 +105,10 @@
         return tuple(turned), tuple(logs)
 
     zero = jnp.zeros(shape, jnp.float32)
-    return lax.fori_loop(0, count, step, (mats, tuple(zero for _ in mats)))
+    carry = (mats, tuple(zero for _ in mats))
+    for start in range(0, count, segment):
+        carry = lax.fori_loop(start, start + segment, functools.partial(step, start), carry)
+    return carry
 
 
 MESH = pl.DeviceIdType.MESH
@@ -201,7 +186,7 @@
     )(*arrays)
 
 
-def plan_kernel(capacity, first_ref, near_ref, pos_ref, slot_ref, recv_ref, seen_ref):
+def plan_kernel(capacity, first_ref, near_ref, pos_ref, slot_ref, local_ref, seen_ref):
     count, blocks = near_ref.shape[:2]
     me = first_ref[0]
 
@@ -211,34 +196,21 @@
 
     for i in range(count * capacity):
         slot_ref[i] = 3 * blocks
-        recv_ref[i] = -1
-    for i in range(2 * count):
+        local_ref[i] = -1
+    for i in range(count):
         seen_ref[i] = 0
 
     def place_own(b, c):
         for j in range(3):
-            at = position(me, b, j) // blocks
+            row = position(me, b, j)
+            at = row // blocks
             rank = seen_ref[at]
             seen_ref[at] = rank + 1
             slot_ref[at * capacity + rank] = b * 3 + j
+            local_ref[at * capacity + rank] = row % blocks
         return c
 
     lax.fori_loop(0, blocks, place_own, 0)
-
-    def place(i, c):
-        for j in range(3):
-            sender = i // blocks
-            row = position(sender, i % blocks, j)
-
-            @pl.when(row // blocks == me)
-            def _():
-                rank = seen_ref[count + sender]
-                seen_ref[count + sender] = rank + 1
-                recv_ref[sender * capacity + rank] = row % blocks
-
-        return c
-
-    lax.fori_loop(0, count * blocks, place, 0)
 
 
 def plan_slots(first, near, positions, capacity):
@@ -250,7 +222,7 @@
         out_shape=(slots, slots),
         in_specs=[smem] * 3,
         out_specs=(smem, smem),
-        scratch_shapes=[pltpu.SMEM((2 * count,), jnp.int32)],
+        scratch_shapes=[pltpu.SMEM((count,), jnp.int32)],
     )(first, near, positions)
 
 
@@ -300,27 +272,33 @@
     below = lax.broadcasted_iota(jnp.int32, (bs, bs), 0) >= lax.broadcasted_iota(
         jnp.int32, (bs, bs), 1
     )
-    for j in range(3):
-        inverse, _ = sweep(load(j), False)
+    invs = []
+    for j in range(4):
+        low, logs = sweep(load(j))
+        invs.append([jnp.where(below, jnp.concatenate(low[b], axis=0), 0.0) for b in range(nb)])
+        if j == 3:
+            break
         for b in range(nb):
-            p = jnp.concatenate(inverse[b], axis=0)
-            rest = a_ref[b, (j + 1) * bs :, part(j)]
-            scaled = dot(rest, p)
+            scaled = dot_nt(a_ref[b, (j + 1) * bs :, part(j)], invs[j][b])
             for i in range(j + 1, 4):
                 row = scaled[(i - j - 1) * bs : (i - j) * bs]
                 a_ref[b, part(i), (j + 1) * bs : (i + 1) * bs] -= dot_nt(
-                    row, rest[: (i - j) * bs]
+                    row, scaled[: (i - j) * bs]
                 )
             a_ref[b, (j + 1) * bs :, part(j)] = scaled
-    low, logs = sweep(load(3), True)
+            a_ref[b, part(j), part(j)] = invs[j][b]
     for b in range(nb):
-        low_inv = jnp.where(below, jnp.concatenate(low[b], axis=0), 0.0)
-        x2 = a_ref[b, part(3), part(2)]
-        x1 = a_ref[b, part(3), part(1)] - dot(x2, a_ref[b, part(2), part(1)])
-        x0 = (
+        low_inv = invs[3][b]
+        x2 = dot(a_ref[b, part(3), part(2)], a_ref[b, part(2), part(2)])
+        x1 = dot(
+            a_ref[b, part(3), part(1)] - dot(x2, a_ref[b, part(2), part(1)]),
+            a_ref[b, part(1), part(1)],
+        )
+        x0 = dot(
             a_ref[b, part(3), part(0)]
             - dot(x1, a_ref[b, part(1), part(0)])
-            - dot(x2, a_ref[b, part(2), part(0)])
+            - dot(x2, a_ref[b, part(2), part(0)]),
+            a_ref[b, part(0), part(0)],
         )
         g_ref[b, :, part(3)] = low_inv
         for i, x in enumerate((x0, x1, x2)):
@@ -337,7 +315,7 @@
 
 def main_kernel(
     count, depth, capacity,
-    near_ref, pos_ref, slot_ref, recv_ref, points_ref, values_ref, probes_ref,
+    near_ref, pos_ref, slot_ref, local_ref, points_ref, values_ref, probes_ref,
     rem_ref, tri_ref, w_ref, t_ref,
     a_ref, g_ref, wt_all, probes_all, q, z, sp,
     in1s, in1r, in2s, in2r, out1s, out1r, out2s, out2r, e1s, e1r, e2s, e2r,
@@ -361,6 +339,7 @@
         return to_peers("probe", depth, source, target, zsem.at[2 * i], zsem.at[2 * i + 1])
 
     greet((("rows", count), ("probe", depth)))
+    line = lax.broadcasted_iota(jnp.int32, (cols, bs), 0)
     here = pl.ds(me * blocks, blocks)
     probe_copies = over_rows(0, lambda peer: probes_ref, probes_all.at[here])
     keep = pltpu.make_async_copy(probes_ref, probes_all.at[here], own_sem)
@@ -420,15 +399,20 @@
             for k in range(capacity):
                 sb[d, k] = sp[slot_ref[d * capacity + k]]
             sb[d, capacity] = energy
+            tile = jnp.full((cols, bs), -1, jnp.int32)
+            for k in range(capacity):
+                tile = jnp.where(line == k, local_ref[d * capacity + k], tile)
+            sb[d, capacity + 1] = tile.astype(jnp.float32)
         copies = over_rows(i, lambda peer: sb.at[peer], rb.at[me])
         rb[me] = sb[me]
         wait_all(copies)
         sums = [outr[b // nb, b % nb, :, 3 * bs :] for b in range(blocks)]
         energy = jnp.zeros((cols, bs), jnp.float32)
         for d in range(count):
+            tile = rb[d, capacity + 1]
             for k in range(capacity):
                 value = rb[d, k]
-                local = recv_ref[d * capacity + k]
+                local = jnp.broadcast_to(tile[k : k + 1, :], (cols, bs))
                 for b in range(blocks):
                     sums[b] = sums[b] + jnp.where(local == b, value, 0.0)
             energy = energy + rb[d, capacity]
@@ -472,7 +456,7 @@
     dma = pltpu.SemaphoreType.DMA
     wide = pltpu.VMEM((depth, nb, cols, 4 * bs), f32)
     small = pltpu.VMEM((depth, cols, bs), f32)
-    exchange = pltpu.VMEM((count, capacity + 1, cols, bs), f32)
+    exchange = pltpu.VMEM((count, capacity + 2, cols, bs), f32)
     return pl.pallas_call(
         functools.partial(main_kernel, count, depth, capacity),
         out_shape=(

time: 133 us -> 123 us (0.925)
  Pallas kernels: 124 us -> 114 us
    pallas_call x1, Pallas kernels: 109 us -> 104 us  [main_call(): pl.pallas_call(functools.partial(main_kernel, count, depth, capacity), ou...]
    pallas_call x1, Pallas kernels: 6.26 us -> 2.27 us  [plan_slots(): pl.pallas_call(functools.partial(plan_kernel, capacity), out_shape=(slots...]
where the time goes in v3:
time: 123 us; the launch traced here: 121 us
  Pallas kernels  114 us (93%)
  local copies, waits for them, and re-layouts  6.01 us (5%)
    pallas_call x1, Pallas kernels, main_call(): pl.pallas_call(functools.partial(main_kernel, count, depth, capacity), ou...  104 us
    pallas_call x1, Pallas kernels, gather_rows(): pl.pallas_call(functools.partial(gather_kernel, count), out_shape=[jax.Sh...  7.98 us
    unnamed x11, local copies, waits for them, and re-layouts  4.7 us

profile of v3, /device:TPU:9, one launch (start us, length us, event | category | flops | bytes accessed | tf_op | source)
XLA Modules:
  0.0 120.6 jit_solution(11735310226802141087)
XLA Ops:
  0.6 0.0 copy-start
  0.6 1.3 %copy.13.refs_2_ = s32[8,3]{1,0:T(8,128)} copy(s32[8,3]{0,1:T(4,128)} %param.8) | data formatting | bytes 192 | tf_op args[3]
  2.0 0.0 copy-done
  2.0 0.6 copy.12.refs_0_
  2.6 8.0 %shard_map.84 = (f32[8,8,3,128]{3,2,1,0:T(4,128)}, f32[8,8,128]{2,1,0:T(8,128)}, s32[8,8,3]{2,1,0:T(8,128)}, s32[8,1,8]{2,1,0:T(1,128)}) custom-call(f32[8,3,128]{2,1,0:T(4,128)} %copy.12.refs_0_, f32[8,128]{1,0:T(8,128)} %refs_1_.1, s32[8,3]{1,0:T(8,128)} %copy.13.refs_2_, s32[1,8]{1,0:T(1,128)} %bitcast.4), custom_call_target="tpu_custom_call" | custom-call | tf_op jit(solution)/shard_map/pallas_call | solution.py:175
  10.6 2.3 %shard_map.85 = (s32[48]{0:T(128)}, s32[48]{0:T(128)}) custom-call(s32[1]{0:T(128)} %bitcast.1.first_ref, s32[8,8,3]{2,1,0:T(8,128)} %get-tuple-element.14.near_ref, s32[8,1,8]{2,1,0:T(1,128)} %get-tuple-element.15.pos_ref), custom_call_target="tpu_custom_call" | custom-call | tf_op jit(solution)/shard_map/pallas_call | solution.py:220
  12.9 103.6 %shard_map.86 = (f32[8,16,128]{2,1,0:T(8,128)}, f32[16,128]{1,0:T(8,128)}, f32[8,128]{1,0:T(8,128)}, f32[8,128]{1,0:T(8,128)}) custom-call(s32[8,8,3]{2,1,0:T(8,128)} %get-tuple-element.14.near_ref, s32[8,1,8]{2,1,0:T(1,128)} %get-tuple-element.15.pos_ref, s32[48]{0:T(128)} %get-tuple-element.16.slot_ref, s32[48]{0:T(128)} %get-tuple-element.17.local_ref, ...), custom_call_target="tpu_custom_call" | custom-call | tf_op jit(solution)/shard_map/pallas_call | solution.py:460
  116.5 0.0 copy-start.1
  116.5 1.3 %slice_reduce_fusion = f32[8]{0:T(128)} fusion(f32[8,128]{1,0:T(8,128)} %get-tuple-element.21), kind=kLoop, calls=%fused_computation | loop fusion | bytes 64 | tf_op jit(solution)/shard_map/slice | solution.py:501
  117.8 0.0 copy-done.1
  117.8 0.0 copy-start.2
  117.8 0.7 copy.14
  118.5 0.0 copy-done.2
  118.5 0.6 copy.17
  119.1 1.5 %copy.18 = f32[8,16,128]{2,1,0:T(8,128)} copy(f32[8,16,128]{2,1,0:T(8,128)} %get-tuple-element.39) | data formatting | bytes 131072
Async XLA Ops:
  0.6 1.4 %copy-start = (f32[8,3,128]{2,0,1:T(8,128)S(1)}, f32[8,3,128]{2,0,1:T(8,128)}, u32[]{:S(2)}) copy-start(f32[8,3,128]{2,0,1:T(8,128)} %param.5) | copy-start | bytes 36868
  116.5 1.3 %copy-start.1 = (f32[16,128]{1,0:T(8,128)S(1)}, f32[16,128]{1,0:T(8,128)}, u32[]{:S(2)}) copy-start(f32[16,128]{1,0:T(8,128)} %get-tuple-element.22) | copy-start | bytes 24580
  117.8 0.7 copy-start.2
